TPU v7x, 32 devices: a whole 2x2x4 slice. The times are simulated.
32 devices in a mesh: section: 4 (over y, x), feat: 4 (over z), dp: 2 (over core).
Axes of the slice: x: 2, y: 2, z: 4, core: 2. Of those that a mesh axis runs over, the one named last changes fastest.
Arguments:
- section_outputs: bfloat16 [4, 1024, 4608], P('section', 'dp', 'feat'), may hold values from -6 to 6
- enc_weight: bfloat16 [4608, 16384], P('dp', ('section', 'feat')), may hold values from -0.09375 to 0.09375
- enc_bias: float32 [16384], P(('section', 'feat')), may hold values from -3 to 3
- thresholds: int32 [16384], P(('section', 'feat')), may hold values from 0 to 7
- dec_weight: bfloat16 [16384, 4608], P(('section', 'feat'), 'dp'), may hold values from -0.09375 to 0.09375
- dec_bias: float32 [4608], replicated, may hold values from -3 to 3
- enc_moment: float32 [4608, 16384], P('dp', ('section', 'feat')), may hold values from -2 to 2
- enc_second: float32 [4608, 16384], P('dp', ('section', 'feat')), may hold values from 0.01 to 1
- dec_moment: float32 [16384, 4608], P(('section', 'feat'), 'dp'), may hold values from -2 to 2
- dec_second: float32 [16384, 4608], P(('section', 'feat'), 'dp'), may hold values from 0.01 to 1
Outputs:
- enc_update: bfloat16 [4608, 16384], P('dp', ('section', 'feat'))
- enc_moment_new: float32 [4608, 16384], P('dp', ('section', 'feat'))
- enc_second_new: float32 [4608, 16384], P('dp', ('section', 'feat'))
- dec_update: bfloat16 [16384, 4608], P(('section', 'feat'), 'dp')
- dec_moment_new: float32 [16384, 4608], P(('section', 'feat'), 'dp')
- dec_second_new: float32 [16384, 4608], P(('section', 'feat'), 'dp')
All inputs are finite; a program needn't handle non-finite values.
Results may differ from a plain program's by a relative error of at most 0.0055.
The roundings to bfloat16 on the way count: a program that leaves them out, or rounds other values in their place, can miss the bound.
Values may be sent and summed in bfloat16 or wider, within the bound.
No kernel may reach another device: no remote copies, remote signals or barrier semaphores. Data moves between devices by JAX's collectives and lax.ppermute only.
A program may use at most 256 MiB of HBM per device.

v0:
```python
import math
import jax
import jax.numpy as jnp
from jax import lax
from jax.sharding import PartitionSpec as P

band = 0.1
level_step = 0.25
beta_first = 0.9
beta_second = 0.999
fix_first = 1.0 - (0.9**50) ** 2
fix_second = 1.0 - (0.999**50) ** 2
epsilon = 1e-08


def adam_moves(moment, second, grads):
    moment_new = beta_first * moment + (1.0 - beta_first) * grads
    second_new = beta_second * second + (1.0 - beta_second) * grads * grads
    update = (moment_new / fix_first / (jnp.sqrt(second_new / fix_second) + epsilon)).astype(
        jnp.bfloat16
    )
    return (update, moment_new, second_new)


def on_device(
    section_outputs,
    enc_weight,
    enc_bias,
    thresholds,
    dec_weight,
    dec_bias,
    enc_moment,
    enc_second,
    dec_moment,
    dec_second,
):
    own_part = section_outputs[0].astype(jnp.float32)
    summed = lax.psum(own_part, "section").astype(jnp.bfloat16)
    resid = lax.all_gather(summed, "feat", axis=1, tiled=True)
    tok_rows = resid.shape[0]
    token_total = tok_rows * lax.axis_size("dp")
    columns = resid
    preact = (
        jnp.dot(
            columns,
            lax.all_gather(enc_weight, "dp", axis=0, tiled=True),
            preferred_element_type=jnp.float32,
        )
        + enc_bias
    )
    theta = level_step * (thresholds.astype(jnp.float32) + 1.0)
    opened = jax.nn.sigmoid((preact - theta) / band)
    codes = (preact * opened).astype(jnp.bfloat16)
    dec_full = lax.all_gather(dec_weight, "dp", axis=1, tiled=True)
    groups = lax.axis_size(("section", "feat"))
    position = lax.axis_index(("section", "feat"))
    span = tok_rows // groups
    recon = lax.psum_scatter(
        jnp.dot(codes, dec_full, preferred_element_type=jnp.float32),
        ("section", "feat"),
        scatter_dimension=0,
        tiled=True,
    )
    first = position * span
    target = lax.dynamic_slice_in_dim(resid, first, span, 0).astype(jnp.float32)
    error_part = ((recon + dec_bias - target) / math.sqrt(token_total)).astype(jnp.bfloat16)
    grad_out = lax.all_gather(error_part, ("section", "feat"), axis=0, tiled=True)
    dec_whole = lax.dot_general(
        codes, grad_out, (((0,), (0,)), ((), ())), preferred_element_type=jnp.float32
    )
    dec_grad = lax.psum_scatter(dec_whole, "dp", scatter_dimension=1, tiled=True)
    back = lax.dot_general(
        grad_out, dec_full, (((1,), (1,)), ((), ())), preferred_element_type=jnp.float32
    )
    pre_grad = (back * (opened + preact * opened * (1.0 - opened) / band)).astype(jnp.bfloat16)
    columns = resid
    enc_grad = lax.psum_scatter(
        lax.dot_general(
            columns, pre_grad, (((0,), (0,)), ((), ())), preferred_element_type=jnp.float32
        ),
        "dp",
        scatter_dimension=0,
        tiled=True,
    )
    enc_update, enc_moment_new, enc_second_new = adam_moves(enc_moment, enc_second, enc_grad)
    dec_update, dec_moment_new, dec_second_new = adam_moves(dec_moment, dec_second, dec_grad)
    return (enc_update, enc_moment_new, enc_second_new, dec_update, dec_moment_new, dec_second_new)


def solution(mesh):
    return jax.shard_map(
        on_device,
        mesh=mesh,
        in_specs=(
            P("section", "dp", "feat"),
            P("dp", ("section", "feat")),
            P(("section", "feat")),
            P(("section", "feat")),
            P(("section", "feat"), "dp"),
            P(),
            P("dp", ("section", "feat")),
            P("dp", ("section", "feat")),
            P(("section", "feat"), "dp"),
            P(("section", "feat"), "dp"),
        ),
        out_specs=(
            P("dp", ("section", "feat")),
            P("dp", ("section", "feat")),
            P("dp", ("section", "feat")),
            P(("section", "feat"), "dp"),
            P(("section", "feat"), "dp"),
            P(("section", "feat"), "dp"),
        ),
        check_vma=False,
    )
```

profile of v0, /device:TPU:0, one launch (start us, length us, event | category | flops | bytes accessed | tf_op | source)
XLA Modules:
  0.0 630.2 jit_solution(8954610613970382083)
XLA Ops:
  7.2 1.4 bitcast_convert_fusion
  8.6 86.1 %all-reduce.1 = bf16[512,1152]{1,0:T(8,128)(2,1)} all-reduce(f32[512,1152]{1,0:T(8,128)S(1)} %bitcast_convert_fusion), channel_id=1, replica_groups=mesh['section'=4,'feat'=4,'dp'=2] {'section'}, use_global_device_ids=true, to_apply=%region_0.0 | all-reduce | flops 589824 | bytes 3538944 | tf_op jit(solution)/shard_map/psum | solution.py:38
  94.9 0.7 all-gather.7.cloned.1.call-update
  95.6 0.7 all-gather.9.cloned.1.call-update
  96.4 87.7 %all-gather.5.cloned.1.call-done = bf16[512,4608]{1,0:T(8,128)(2,1)} async-done(((bf16[512,1152]{1,0:T(8,128)(2,1)}), bf16[512,4608]{1,0:T(8,128)(2,1)}) %all-gather.5.cloned.1.call-update) | async-done | bytes 4718608 | tf_op jit(solution)/shard_map/all_gather | solution.py:39
  184.1 21.6 %all-gather.7.cloned.1.call-done = bf16[4608,1024]{1,0:T(8,128)(2,1)} async-done(((bf16[2304,1024]{1,0:T(8,128)(2,1)}), bf16[4608,1024]{1,0:T(8,128)(2,1)}) %all-gather.7.cloned.1.call-update) | async-done | bytes 9437200 | tf_op jit(solution)/shard_map/all_gather | solution.py:46
  205.7 9.0 %fusion.15 = f32[512,1024]{1,0:T(8,128)S(1)} fusion(bf16[512,4608]{1,0:T(8,128)(2,1)} %all-gather.5.cloned.1.call-done, bf16[4608,1024]{1,0:T(8,128)(2,1)} %all-gather.7.cloned.1.call-done), kind=kOutput, calls=%fused_computation.24 | convolution fusion | flops 4831838208 | bytes 16252928 | tf_op jit(solution)/shard_map/dot_general | solution.py:44
  214.7 15.4 %all-gather.9.cloned.1.call-done = bf16[1024,4608]{1,0:T(8,128)(2,1)} async-done(((bf16[1024,2304]{1,0:T(8,128)(2,1)}), bf16[1024,4608]{1,0:T(8,128)(2,1)}) %all-gather.9.cloned.1.call-update) | async-done | bytes 9437200 | tf_op jit(solution)/shard_map/all_gather | solution.py:54
  230.1 11.3 %fusion.11 = f32[512,4608]{1,0:T(8,128)} fusion(bf16[1024,4608]{1,0:T(8,128)(2,1)} %all-gather.9.cloned.1.call-done, f32[512,1024]{1,0:T(8,128)S(1)} %fusion.15, f32[1024]{0:T(1024)S(1)} %add_multiply_fusion.1, f32[1024]{0:T(1024)S(1)} %copy-done), kind=kOutput, calls=%fused_computation.23 | convolution fusion | flops 4836032512 | bytes 20979712 | tf_op jit(solution)/shard_map/dot_general | solution.py:59
  241.4 0.0 all-gather.11.cloned.1.call-start
  241.4 172.9 %reduce-scatter.4.cloned.1.call-done = f32[32,4608]{1,0:T(8,128)} async-done(((f32[512,4608]{1,0:T(8,128)}), f32[32,4608]{1,0:T(8,128)}) %reduce-scatter.4.cloned.1.call-update) | async-done | bytes 589840 | tf_op jit(solution)/shard_map/reduce_scatter | solution.py:58
  414.3 1.9 multiply_convert_fusion.1
  416.3 0.0 reduce-scatter.6.cloned.1.call-start
  416.3 80.0 %all-gather.11.cloned.1.call-done = bf16[512,4608]{1,0:T(8,128)(2,1)} async-done(((bf16[32,4608]{1,0:T(8,128)(2,1)}), bf16[512,4608]{1,0:T(8,128)(2,1)}) %all-gather.11.cloned.1.call-update) | async-done | bytes 4718608 | tf_op jit(solution)/shard_map/all_gather | solution.py:67
  496.3 19.5 %convolution_bitcast_fusion = f32[4608,1024]{0,1:T(8,128)} fusion(bf16[512,4608]{1,0:T(8,128)(2,1)} %all-gather.5.cloned.1.call-done, f32[512,1024]{1,0:T(8,128)S(1)} %fusion.15, bf16[512,4608]{1,0:T(8,128)(2,1)} %all-gather.11.cloned.1.call-done, bf16[1024,4608]{1,0:T(8,128)(2,1)} %all-gather.9.cloned.1.call-done, f32[1024]{0:T(1024)S(1)} %add_multiply_fusion.1, ...), kind=kOutput, calls=%fused_computation.2 | convolution fusion | flops 9670492160 | bytes 39854080 | tf_op jit(solution)/shard_map/dot_general | solution.py:78
  515.9 0.2 reduce-scatter.8.cloned.1.call-start
  516.1 16.0 %fusion.9 = f32[1024,4608]{1,0:T(8,128)} fusion(bf16[512,4608]{1,0:T(8,128)(2,1)} %all-gather.11.cloned.1.call-done, f32[512,1024]{1,0:T(8,128)S(1)} %fusion.15, f32[1024]{0:T(1024)S(1)} %add_multiply_fusion.1, f32[1024]{0:T(1024)S(1)} %copy-done), kind=kOutput, calls=%fused_computation.22 | convolution fusion | flops 4836032512 | bytes 25698304 | tf_op jit(solution)/shard_map/dot_general | solution.py:68
  532.2 10.7 %copy.16 = f32[2304,1024]{0,1:T(8,128)} copy(f32[2304,1024]{1,0:T(8,128)} %param.16) | data formatting | bytes 18874368 | tf_op args[6]
  542.9 9.7 %copy.17 = f32[2304,1024]{0,1:T(8,128)} copy(f32[2304,1024]{1,0:T(8,128)} %param.17) | data formatting | bytes 18874368 | tf_op args[7]
  552.6 25.6 %divide_convert_fusion.1 = (bf16[2304,1024]{0,1:T(8,128)(2,1)}, f32[2304,1024]{0,1:T(8,128)}, f32[2304,1024]{0,1:T(8,128)}) fusion(f32[2304,1024]{0,1:T(8,128)} %reduce-scatter.6.cloned.1.call-done, f32[2304,1024]{0,1:T(8,128)} %copy.16, f32[2304,1024]{0,1:T(8,128)} %copy.17), kind=kLoop, calls=%fused_computation.7 | loop fusion | flops 28311552 | bytes 51904512 | tf_op jit(solution)/shard_map/convert_element_type | solution.py:19
  578.2 6.6 %copy.18 = bf16[2304,1024]{1,0:T(8,128)(2,1)} copy(bf16[2304,1024]{0,1:T(8,128)(2,1)} %get-tuple-element.15) | data formatting | bytes 9437184
  584.8 9.6 %copy.19 = f32[2304,1024]{1,0:T(8,128)} copy(f32[2304,1024]{0,1:T(8,128)} %get-tuple-element.16) | data formatting | bytes 18874368
  594.4 9.6 %copy.20 = f32[2304,1024]{1,0:T(8,128)} copy(f32[2304,1024]{0,1:T(8,128)} %get-tuple-element.17) | data formatting | bytes 18874368
  604.0 19.4 %divide_convert_fusion = (bf16[1024,2304]{1,0:T(8,128)(2,1)}, f32[1024,2304]{1,0:T(8,128)}, f32[1024,2304]{1,0:T(8,128)}) fusion(f32[1024,2304]{1,0:T(8,128)} %reduce-scatter.8.cloned.1.call-done, f32[1024,2304]{1,0:T(8,128)} %param.18, f32[1024,2304]{1,0:T(8,128)} %param.19), kind=kLoop, calls=%fused_computation.5 | loop fusion | flops 28311552 | bytes 51904512 | tf_op jit(solution)/shard_map/convert_element_type | solution.py:19
  (18 shorter events, 0.3 us)
Async XLA Ops:
  7.2 176.9 %all-gather.5.cloned.1.call-start = ((), (), s32[]{:S(2)}) async-start(), calls=%async_computation.3 | async-start | bytes 5898240 | tf_op jit(solution)/shard_map/all_gather | solution.py:39
  94.8 1.5 copy-start.2
  94.8 110.9 %all-gather.7.cloned.1.call-start = ((), (), s32[]{:S(2)}) async-start(), calls=%async_computation.4 | async-start | bytes 14155776 | tf_op jit(solution)/shard_map/all_gather | solution.py:46
  95.6 134.5 %all-gather.9.cloned.1.call-start = ((), (), s32[]{:S(2)}) async-start(), calls=%async_computation.5 | async-start | bytes 14155776 | tf_op jit(solution)/shard_map/all_gather | solution.py:54
  96.3 318.0 %reduce-scatter.4.cloned.1.call-start = ((), (), s32[]{:S(2)}) async-start(), calls=%async_computation.6 | async-start | bytes 10027008 | tf_op jit(solution)/shard_map/reduce_scatter | solution.py:58
  96.4 133.7 %copy-start = (f32[1024]{0:T(1024)S(1)}, f32[1024]{0:T(1024)}, u32[]{:S(2)}) copy-start(f32[1024]{0:T(1024)} %param.12) | copy-start | bytes 12292
  241.3 173.0 %copy-start.1 = (f32[4608]{0:T(1024)S(1)}, f32[4608]{0:T(1024)}, u32[]{:S(2)}) copy-start(f32[4608]{0:T(1024)} %param.15) | copy-start | bytes 55300
  241.4 255.0 %all-gather.11.cloned.1.call-start = ((), (), s32[]{:S(2)}) async-start(), calls=%async_computation.7 | async-start | bytes 5013504 | tf_op jit(solution)/shard_map/all_gather | solution.py:67
  416.3 136.4 %reduce-scatter.6.cloned.1.call-start = ((), (), s32[]{:S(2)}) async-start(), calls=%async_computation.8 | async-start | bytes 28311552 | tf_op jit(solution)/shard_map/reduce_scatter | solution.py:77
  515.9 88.1 %reduce-scatter.8.cloned.1.call-start = ((), (), s32[]{:S(2)}) async-start(), calls=%async_computation.9 | async-start | bytes 28311552 | tf_op jit(solution)/shard_map/reduce_scatter | solution.py:71
Sparse Core Ops, SparseCore 0:
  94.9 89.0 all-gather.4
  185.6 20.0 all-gather.6
  207.3 22.7 all-gather.8
  241.5 172.7 reduce-scatter.3
  417.5 78.8 all-gather.10
  516.0 25.1 reduce-scatter.5
  543.5 27.7 reduce-scatter.7
where the time goes:
time: 631 us; the launch traced here: 630 us
  waiting for transfers between devices  379 us (60%)
  blocking collectives  86.1 us (14%)
  matrix products  55.8 us (9%)
  other arithmetic  48.4 us (8%)
  local copies, waits for them, and re-layouts  46.2 us (7%)
  between operations  14.2 us (2%)
    reduce_scatter x1, waiting for transfers between devices, on_device(): lax.psum_scatter(jnp.dot(codes, dec_full, preferred_element_type=jnp.floa...  173 us
    all_gather x1, waiting for transfers between devices, on_device(): resid = lax.all_gather(summed, 'feat', axis=1, tiled=True)  87.7 us
    psum x1, blocking collectives, on_device(): summed = lax.psum(own_part, 'section').astype(jnp.bfloat16)  86.1 us
    all_gather x1, waiting for transfers between devices, on_device(): lax.all_gather(error_part, ('section', 'feat'), axis=0, tiled=True)  80 us
    unnamed x11, local copies, waits for them, and re-layouts  46.2 us
    convert_element_type x2, other arithmetic, adam_moves(): (moment_new / fix_first / (jnp.sqrt(second_new / fix_second) + epsilon))....  45 us
    all_gather x1, waiting for transfers between devices, on_device(): lax.all_gather(enc_weight, 'dp', axis=0, tiled=True)  21.6 us
    dot_general x1, matrix products, on_device(): lax.dot_general(columns, pre_grad, (((0,), (0,)), ((), ())), preferred_el...  19.5 us
  transfers between devices with their start and end apart: 7, of which 5 were waited for; matrix products, arithmetic and copies ran while one was open for 15% of the time, Pallas kernels for 0%

commit v1 on v0

--- a/solution.py
+++ b/solution.py
@@ -35,7 +35,7 @@
     dec_second,
 ):
     own_part = section_outputs[0].astype(jnp.float32)
-    summed = lax.psum(own_part, "section").astype(jnp.bfloat16)
+    summed = jnp.sum(lax.all_gather(own_part, "section"), axis=0).astype(jnp.bfloat16)
     resid = lax.all_gather(summed, "feat", axis=1, tiled=True)
     tok_rows = resid.shape[0]
     token_total = tok_rows * lax.axis_size("dp")

time: 631 us -> 607 us (0.962)
  waiting for transfers between devices: 379 us -> 484 us
  blocking collectives: 86.1 us -> 0 us
  local copies, waits for them, and re-layouts: 46.2 us -> 0.04 us
    all_gather x0 -> x1, waiting for transfers between devices: none -> 98.5 us  [on_device(): lax.all_gather(own_part, 'section')]
    psum x1 -> x0, blocking collectives: 86.1 us -> none  [on_device(): summed = lax.psum(own_part, 'section').astype(jnp.bfloat16)]
    unnamed x11 -> x6, local copies, waits for them, and re-layouts: 46.2 us -> 0.04 us
    reduce_scatter x1, waiting for transfers between devices: 0.01 us -> 7.96 us  [on_device(): lax.psum_scatter(lax.dot_general(columns, pre_grad, (((0,), (0,)), ((), (...]
  transfers between devices with their start and end apart: 7 -> 8, of which waited for: 5 -> 8; matrix products, arithmetic and copies ran while one was open for 15% -> 10% of each run, Pallas kernels for 0% -> 0%
where the time goes in v1:
time: 607 us
  waiting for transfers between devices  484 us (80%)
  matrix products  55 us (9%)
  other arithmetic  52.7 us (9%)
  between operations  14.2 us (2%)
    reduce_scatter x1, waiting for transfers between devices, on_device(): lax.psum_scatter(jnp.dot(codes, dec_full, preferred_element_type=jnp.floa...  173 us
    all_gather x1, waiting for transfers between devices, on_device(): lax.all_gather(own_part, 'section')  98.5 us
    all_gather x1, waiting for transfers between devices, on_device(): resid = lax.all_gather(summed, 'feat', axis=1, tiled=True)  92.8 us
    all_gather x1, waiting for transfers between devices, on_device(): lax.all_gather(error_part, ('section', 'feat'), axis=0, tiled=True)  80.2 us
    convert_element_type x2, other arithmetic, adam_moves(): (moment_new / fix_first / (jnp.sqrt(second_new / fix_second) + epsilon))....  42.4 us
    dot_general x1, matrix products, on_device(): lax.dot_general(columns, pre_grad, (((0,), (0,)), ((), ())), preferred_el...  23.3 us
    all_gather x1, waiting for transfers between devices, on_device(): lax.all_gather(enc_weight, 'dp', axis=0, tiled=True)  17 us
    all_gather x1, waiting for transfers between devices, on_device(): dec_full = lax.all_gather(dec_weight, 'dp', axis=1, tiled=True)  12.5 us
  transfers between devices with their start and end apart: 8, of which 8 were waited for; matrix products, arithmetic and copies ran while one was open for 10% of the time, Pallas kernels for 0%

profile of v1, /device:TPU:0, one launch (start us, length us, event | category | flops | bytes accessed | tf_op | source)
XLA Modules:
  0.0 606.9 jit_solution(7311320905511182496)
XLA Ops:
  7.2 2.8 convert_element_type.28
  10.1 0.0 all-gather.10.cloned.1.call-start
  10.1 0.7 all-gather.10.cloned.1.call-update
  10.9 98.5 %all-gather.6.cloned.1.call-done = f32[4,512,1152]{2,1,0:T(8,128)} async-done(((f32[1,512,1152]{2,1,0:T(8,128)}), f32[4,512,1152]{2,1,0:T(8,128)}) %all-gather.6.cloned.1.call-update) | async-done | bytes 9437200 | tf_op jit(solution)/shard_map/all_gather | solution.py:38
  109.3 5.6 reduce_sum.9
  114.9 0.0 all-gather.12.cloned.1.call-start
  115.0 0.5 all-gather.12.cloned.1.call-update
  115.6 17.0 %all-gather.10.cloned.1.call-done = bf16[4608,1024]{1,0:T(8,128)(2,1)} async-done(((bf16[2304,1024]{1,0:T(8,128)(2,1)}), bf16[4608,1024]{1,0:T(8,128)(2,1)}) %all-gather.10.cloned.1.call-update) | async-done | bytes 9437200 | tf_op jit(solution)/shard_map/all_gather | solution.py:46
  132.6 92.8 %all-gather.8.cloned.1.call-done = bf16[512,4608]{1,0:T(8,128)(2,1)} async-done(((bf16[512,1152]{1,0:T(8,128)(2,1)}), bf16[512,4608]{1,0:T(8,128)(2,1)}) %all-gather.8.cloned.1.call-update) | async-done | bytes 4718608 | tf_op jit(solution)/shard_map/all_gather | solution.py:39
  225.3 9.0 %fusion.16 = f32[512,1024]{1,0:T(8,128)S(1)} fusion(bf16[512,4608]{1,0:T(8,128)(2,1)} %all-gather.8.cloned.1.call-done, bf16[4608,1024]{1,0:T(8,128)(2,1)} %all-gather.10.cloned.1.call-done), kind=kOutput, calls=%fused_computation.23 | convolution fusion | flops 4831838208 | bytes 16252928 | tf_op jit(solution)/shard_map/dot_general | solution.py:44
  234.3 12.5 %all-gather.12.cloned.1.call-done = bf16[1024,4608]{1,0:T(8,128)(2,1)} async-done(((bf16[1024,2304]{1,0:T(8,128)(2,1)}), bf16[1024,4608]{1,0:T(8,128)(2,1)}) %all-gather.12.cloned.1.call-update) | async-done | bytes 9437200 | tf_op jit(solution)/shard_map/all_gather | solution.py:54
  246.8 11.2 %fusion.12 = f32[512,4608]{1,0:T(8,128)} fusion(bf16[1024,4608]{1,0:T(8,128)(2,1)} %all-gather.12.cloned.1.call-done, f32[512,1024]{1,0:T(8,128)S(1)} %fusion.16, f32[1024]{0:T(1024)S(1)} %add_multiply_fusion.1, f32[1024]{0:T(1024)S(1)} %copy-done), kind=kOutput, calls=%fused_computation.22 | convolution fusion | flops 4836032512 | bytes 20979712 | tf_op jit(solution)/shard_map/dot_general | solution.py:59
  258.0 0.0 all-gather.14.cloned.1.call-start
  258.1 172.6 %reduce-scatter.4.cloned.1.call-done = f32[32,4608]{1,0:T(8,128)} async-done(((f32[512,4608]{1,0:T(8,128)}), f32[32,4608]{1,0:T(8,128)}) %reduce-scatter.4.cloned.1.call-update) | async-done | bytes 589840 | tf_op jit(solution)/shard_map/reduce_scatter | solution.py:58
  430.7 1.9 multiply_convert_fusion.1
  432.6 0.0 reduce-scatter.8.cloned.1.call-start
  432.7 80.2 %all-gather.14.cloned.1.call-done = bf16[512,4608]{1,0:T(8,128)(2,1)} async-done(((bf16[32,4608]{1,0:T(8,128)(2,1)}), bf16[512,4608]{1,0:T(8,128)(2,1)}) %all-gather.14.cloned.1.call-update) | async-done | bytes 4718608 | tf_op jit(solution)/shard_map/all_gather | solution.py:67
  512.9 11.5 %fusion.10 = f32[1024,4608]{1,0:T(8,128)} fusion(bf16[512,4608]{1,0:T(8,128)(2,1)} %all-gather.14.cloned.1.call-done, f32[512,1024]{1,0:T(8,128)S(1)} %fusion.16, f32[1024]{0:T(1024)S(1)} %add_multiply_fusion.1, f32[1024]{0:T(1024)S(1)} %copy-done), kind=kOutput, calls=%fused_computation.21 | convolution fusion | flops 4836032512 | bytes 25698304 | tf_op jit(solution)/shard_map/dot_general | solution.py:68
  524.4 0.2 reduce-scatter.6.cloned.1.call-start
  524.7 23.3 %fusion.3 = f32[4608,1024]{1,0:T(8,128)} fusion(bf16[512,4608]{1,0:T(8,128)(2,1)} %all-gather.8.cloned.1.call-done, f32[512,1024]{1,0:T(8,128)S(1)} %fusion.16, bf16[512,4608]{1,0:T(8,128)(2,1)} %all-gather.14.cloned.1.call-done, bf16[1024,4608]{1,0:T(8,128)(2,1)} %all-gather.12.cloned.1.call-done, f32[1024]{0:T(1024)S(1)} %add_multiply_fusion.1, ...), kind=kOutput, calls=%fused_computation.12 | convolution fusion | flops 9670492160 | bytes 39854080 | tf_op jit(solution)/shard_map/dot_general | solution.py:78
  547.9 1.8 reduce-scatter.8.cloned.1.call-done
  549.7 22.2 %divide_convert_fusion = (bf16[1024,2304]{1,0:T(8,128)(2,1)}, f32[1024,2304]{1,0:T(8,128)}, f32[1024,2304]{1,0:T(8,128)}) fusion(f32[1024,2304]{1,0:T(8,128)} %reduce-scatter.8.cloned.1.call-done, f32[1024,2304]{1,0:T(8,128)} %param.18, f32[1024,2304]{1,0:T(8,128)} %param.19), kind=kLoop, calls=%fused_computation.4 | loop fusion | flops 28311552 | bytes 51904512 | tf_op jit(solution)/shard_map/convert_element_type | solution.py:19
  572.0 8.0 %reduce-scatter.6.cloned.1.call-done = f32[2304,1024]{1,0:T(8,128)} async-done(((f32[4608,1024]{1,0:T(8,128)}), f32[2304,1024]{1,0:T(8,128)}) %reduce-scatter.6.cloned.1.call-update) | async-done | bytes 9437200 | tf_op jit(solution)/shard_map/reduce_scatter | solution.py:77
  579.9 20.1 %divide_convert_fusion.1 = (bf16[2304,1024]{1,0:T(8,128)(2,1)}, f32[2304,1024]{1,0:T(8,128)}, f32[2304,1024]{1,0:T(8,128)}) fusion(f32[2304,1024]{1,0:T(8,128)} %reduce-scatter.6.cloned.1.call-done, f32[2304,1024]{1,0:T(8,128)} %param.16, f32[2304,1024]{1,0:T(8,128)} %param.17), kind=kLoop, calls=%fused_computation.6 | loop fusion | flops 28311552 | bytes 51904512 | tf_op jit(solution)/shard_map/convert_element_type | solution.py:19
  (16 shorter events, 0.3 us)
Async XLA Ops:
  7.2 102.2 %all-gather.6.cloned.1.call-start = ((), (), s32[]{:S(2)}) async-start(), calls=%async_computation.3 | async-start | bytes 11796480 | tf_op jit(solution)/shard_map/all_gather | solution.py:38
  10.1 122.5 %all-gather.10.cloned.1.call-start = ((), (), s32[]{:S(2)}) async-start(), calls=%async_computation.5 | async-start | bytes 14155776 | tf_op jit(solution)/shard_map/all_gather | solution.py:46
  10.8 214.5 %all-gather.8.cloned.1.call-start = ((), (), s32[]{:S(2)}) async-start(), calls=%async_computation.4 | async-start | bytes 5898240 | tf_op jit(solution)/shard_map/all_gather | solution.py:39
  114.9 0.7 copy-start.2
  114.9 131.8 %all-gather.12.cloned.1.call-start = ((), (), s32[]{:S(2)}) async-start(), calls=%async_computation.6 | async-start | bytes 14155776 | tf_op jit(solution)/shard_map/all_gather | solution.py:54
  115.5 315.1 %reduce-scatter.4.cloned.1.call-start = ((), (), s32[]{:S(2)}) async-start(), calls=%async_computation.7 | async-start | bytes 10027008 | tf_op jit(solution)/shard_map/reduce_scatter | solution.py:58
  115.6 131.2 %copy-start = (f32[1024]{0:T(1024)S(1)}, f32[1024]{0:T(1024)}, u32[]{:S(2)}) copy-start(f32[1024]{0:T(1024)} %param.12) | copy-start | bytes 12292
  258.0 172.6 %copy-start.1 = (f32[4608]{0:T(1024)S(1)}, f32[4608]{0:T(1024)}, u32[]{:S(2)}) copy-start(f32[4608]{0:T(1024)} %param.15) | copy-start | bytes 55300
  258.0 254.8 %all-gather.14.cloned.1.call-start = ((), (), s32[]{:S(2)}) async-start(), calls=%async_computation.8 | async-start | bytes 5013504 | tf_op jit(solution)/shard_map/all_gather | solution.py:67
  432.6 117.1 %reduce-scatter.8.cloned.1.call-start = ((), (), s32[]{:S(2)}) async-start(), calls=%async_computation.10 | async-start | bytes 28311552 | tf_op jit(solution)/shard_map/reduce_scatter | solution.py:71
  524.4 55.5 %reduce-scatter.6.cloned.1.call-start = ((), (), s32[]{:S(2)}) async-start(), calls=%async_computation.9 | async-start | bytes 28311552 | tf_op jit(solution)/shard_map/reduce_scatter | solution.py:77
Sparse Core Ops, SparseCore 0:
  10.4 98.9 all-gather.5
  110.9 21.6 all-gather.9
  134.7 90.5 all-gather.7
  226.7 19.9 all-gather.11
  258.2 172.4 reduce-scatter.3
  433.8 78.9 all-gather.13
  524.5 25.1 reduce-scatter.7
  552.0 27.8 reduce-scatter.5
